TPU v7x, 128 devices: a whole 4x4x4 slice. The times are simulated.
128 devices in a mesh: ta: 16 (over y, x_lo, core), ba: 8 (over z, x_hi).
Axes of the slice: x: 4 (x_hi: 2, x_lo: 2; x = x_hi * 2 + x_lo), y: 4, z: 4, core: 2. Of those that a mesh axis runs over, the one named last changes fastest.
Arguments:
- search_block: float32 [16, 2, 4, 3, 32, 512], P(None, None, None, None, 'ta'), may hold values from -140 to 140
- kept_basis: float32 [128, 2, 4, 3, 32, 512], P('ba', None, None, None, 'ta'), may hold values from -4 to 4
- gauge_links: float32 [4, 2, 3, 3, 32, 512], P(None, None, None, None, 'ta'), may hold values from -1 to 1, as said below
- clover_term: float32 [2, 2, 6, 6, 32, 512], P(None, None, None, None, 'ta'), may hold values from -0.5 to 1.3, as said below
Outputs:
- ortho_block: float32 [16, 2, 4, 3, 32, 512], P('ba', None, None, None, 'ta')
- correlations: float32 [2, 128, 16], P(None, 'ba')
Inputs may be any that keep to these rules, and one draw needn't show every extreme that they name: `gauge_links`: every link matrix is special unitary. `clover_term`: each 6x6 block of the clover term is Hermitian.
All inputs are finite; a program needn't handle non-finite values.
Results may differ from a plain program's by a relative error of at most 0.0002.
Values sent between devices are 32-bit elements; how exact they have to be, the bound alone decides.
A program may use at most 128 MiB of HBM per device.

v0:
```python
import jax
import jax.numpy as jnp
import numpy as np
from jax import lax
from jax.sharding import PartitionSpec as P

LS = 8


HOPPING = 0.13
HIGHEST = lax.Precision.HIGHEST


def passed_along(value, axis, steps):
    count = lax.axis_size(axis)
    pairs = [(source, (source + steps) % count) for source in range(count)]
    return lax.ppermute(value, axis, pairs)


def from_everyone(value, axis):
    count = lax.axis_size(axis)
    return lax.all_to_all(
        jnp.broadcast_to(value[None], (count, *value.shape)), axis, 0, 0, tiled=True
    )


def of_everyone(value, axis):
    everything = from_everyone(value, axis)
    return jnp.sum(everything, axis=0)


def gamma_tables():
    gamma_re = np.zeros((4, 4, 4), np.float32)
    gamma_im = np.zeros((4, 4, 4), np.float32)
    gamma_im[0, 0:2, 2:4] = [[0, -1], [-1, 0]]
    gamma_im[0, 2:4, 0:2] = [[0, 1], [1, 0]]
    gamma_re[1, 0:2, 2:4] = [[0, -1], [1, 0]]
    gamma_re[1, 2:4, 0:2] = [[0, 1], [-1, 0]]
    gamma_im[2, 0:2, 2:4] = [[-1, 0], [0, 1]]
    gamma_im[2, 2:4, 0:2] = [[1, 0], [0, -1]]
    gamma_re[3, 0:2, 2:4] = np.eye(2)
    gamma_re[3, 2:4, 0:2] = np.eye(2)
    return (gamma_re, gamma_im)


def gamma_apply(direction, spinor):
    tables_re, tables_im = gamma_tables()
    field_re = spinor[:, 0]
    field_im = spinor[:, 1]
    out_re = jnp.zeros_like(field_re)
    out_im = jnp.zeros_like(field_im)
    if np.any(tables_re[direction]):
        matrix = jnp.asarray(tables_re[direction])
        out_re = out_re + jnp.einsum("as,vsctx->vactx", matrix, field_re, precision=HIGHEST)
        out_im = out_im + jnp.einsum("as,vsctx->vactx", matrix, field_im, precision=HIGHEST)
    if np.any(tables_im[direction]):
        matrix = jnp.asarray(tables_im[direction])
        out_re = out_re - jnp.einsum("as,vsctx->vactx", matrix, field_im, precision=HIGHEST)
        out_im = out_im + jnp.einsum("as,vsctx->vactx", matrix, field_re, precision=HIGHEST)
    return jnp.stack([out_re, out_im], 1)


def gamma_five(spinor):
    return jnp.concatenate([spinor[:, :, :2], -spinor[:, :, 2:]], axis=2)


def colour(link_dir, spinor):
    link_re = link_dir[0][None, None]
    link_im = link_dir[1][None, None]
    field_re = spinor[:, 0][:, :, None]
    field_im = spinor[:, 1][:, :, None]
    out_re = jnp.sum(link_re * field_re - link_im * field_im, axis=3)
    out_im = jnp.sum(link_re * field_im + link_im * field_re, axis=3)
    return jnp.stack([out_re, out_im], 1)


def dagger(link_dir):
    return jnp.stack([link_dir[0].swapaxes(0, 1), -link_dir[1].swapaxes(0, 1)], 0)


def shift_space(values, stride, forward):
    coordinate = jnp.arange(values.shape[-1]) // stride % LS
    if forward:
        return jnp.where(
            coordinate == LS - 1,
            jnp.roll(values, (LS - 1) * stride, axis=-1),
            jnp.roll(values, -stride, axis=-1),
        )
    return jnp.where(
        coordinate == 0,
        jnp.roll(values, -(LS - 1) * stride, axis=-1),
        jnp.roll(values, stride, axis=-1),
    )


def space_hops(spinor, link_field):
    hop_total = jnp.zeros_like(spinor)
    strides = (LS * LS, LS, 1)
    for direction in range(3):
        stride = strides[direction]
        link_dir = link_field[direction]
        ahead_term = colour(link_dir, shift_space(spinor, stride, True))
        behind = colour(
            dagger(shift_space(link_dir, stride, False)), shift_space(spinor, stride, False)
        )
        hop_total = hop_total + (ahead_term + behind) - gamma_apply(direction, ahead_term - behind)
    return hop_total


def clover_apply(clover, spinor):
    vectors = spinor.shape[0]
    pieces = []
    for chiral in range(2):
        chiral_part = spinor[:, :, 2 * chiral : 2 * chiral + 2]
        flat_part = chiral_part.reshape(vectors, 2, 6, chiral_part.shape[-2], chiral_part.shape[-1])
        mat_re = clover[chiral, 0][None]
        mat_im = clover[chiral, 1][None]
        vec_re = flat_part[:, 0][:, None]
        vec_im = flat_part[:, 1][:, None]
        out_re = jnp.sum(mat_re * vec_re - mat_im * vec_im, axis=2)
        out_im = jnp.sum(mat_re * vec_im + mat_im * vec_re, axis=2)
        pieces.append(jnp.stack([out_re, out_im], 1).reshape(chiral_part.shape))
    return jnp.concatenate(pieces, axis=2)


def inner_product(left_re, left_im, right_re, right_im, norm_scale):
    real_part = jnp.einsum("kcn,jcn->kj", left_re, right_re, precision=HIGHEST) + jnp.einsum(
        "kcn,jcn->kj", left_im, right_im, precision=HIGHEST
    )
    imag_part = jnp.einsum("kcn,jcn->kj", left_re, right_im, precision=HIGHEST) - jnp.einsum(
        "kcn,jcn->kj", left_im, right_re, precision=HIGHEST
    )
    return (real_part * norm_scale, imag_part * norm_scale)


def combine_basis(coef_re, coef_im, vec_re, vec_im):
    out_re = jnp.einsum("kj,kcn->jcn", coef_re, vec_re, precision=HIGHEST) - jnp.einsum(
        "kj,kcn->jcn", coef_im, vec_im, precision=HIGHEST
    )
    out_im = jnp.einsum("kj,kcn->jcn", coef_im, vec_re, precision=HIGHEST) + jnp.einsum(
        "kj,kcn->jcn", coef_re, vec_im, precision=HIGHEST
    )
    return (out_re, out_im)


def cholesky_complex(gram_re, gram_im):
    matrix_order = gram_re.shape[0]
    lower_re = jnp.zeros_like(gram_re)
    lower_im = jnp.zeros_like(gram_im)
    index_row = jnp.arange(matrix_order)
    for column in range(matrix_order):
        row_re = lower_re[column]
        row_im = lower_im[column]
        acc_re = gram_re[:, column] - jnp.sum(
            lower_re * row_re[None, :] + lower_im * row_im[None, :], axis=1
        )
        acc_im = gram_im[:, column] - jnp.sum(
            lower_im * row_re[None, :] - lower_re * row_im[None, :], axis=1
        )
        pivot_value = jnp.sqrt(acc_re[column])
        below_mask = index_row > column
        new_re = jnp.where(
            index_row == column, pivot_value, jnp.where(below_mask, acc_re / pivot_value, 0.0)
        )
        new_im = jnp.where(below_mask, acc_im / pivot_value, 0.0)
        lower_re = lower_re.at[:, column].set(new_re)
        lower_im = lower_im.at[:, column].set(new_im)
    return (lower_re, lower_im)


def invert_lower(lower_re, lower_im):
    matrix_order = lower_re.shape[0]
    inverse_re = jnp.zeros_like(lower_re)
    inverse_im = jnp.zeros_like(lower_im)
    index_row = jnp.arange(matrix_order)
    for row_index in range(matrix_order):
        row_re = lower_re[row_index]
        row_im = lower_im[row_index]
        sum_re = jnp.sum(row_re[:, None] * inverse_re - row_im[:, None] * inverse_im, axis=0)
        sum_im = jnp.sum(row_re[:, None] * inverse_im + row_im[:, None] * inverse_re, axis=0)
        unit_row = jnp.where(index_row == row_index, 1.0, 0.0).astype(lower_re.dtype)
        pivot_value = lower_re[row_index, row_index]
        inverse_re = inverse_re.at[row_index].set((unit_row - sum_re) / pivot_value)
        inverse_im = inverse_im.at[row_index].set(-sum_im / pivot_value)
    return (inverse_re, inverse_im)


def per_device(search_block, kept_basis, gauge_links, clover_term):
    time_count = lax.axis_size("ta")
    time_place = lax.axis_index("ta")
    first_sign = jnp.where(time_place == 0, -1.0, 1.0).astype(jnp.float32)
    last_sign = jnp.where(time_place == time_count - 1, -1.0, 1.0).astype(jnp.float32)
    link_time = gauge_links[3]

    def time_hops(spinor):
        diff_half = spinor[:, :, :2] - spinor[:, :, 2:]
        sum_half = spinor[:, :, :2] + spinor[:, :, 2:]
        linked_sum = colour(dagger(link_time), sum_half)
        from_above = passed_along(diff_half[:, :, :, :, 0:1], "ta", -1) * last_sign
        from_below = passed_along(linked_sum[:, :, :, :, -1:], "ta", 1) * first_sign
        ahead_half = colour(
            link_time, jnp.concatenate([diff_half[:, :, :, :, 1:], from_above], axis=4)
        )
        behind_half = jnp.concatenate([from_below, linked_sum[:, :, :, :, :-1]], axis=4)
        return jnp.concatenate([ahead_half + behind_half, behind_half - ahead_half], axis=2)

    def local_dirac(spinor):
        hops = space_hops(spinor, gauge_links) + time_hops(spinor)
        return clover_apply(clover_term, spinor) - HOPPING * hops

    first_apply = local_dirac(search_block)
    applied = gamma_five(local_dirac(gamma_five(first_apply)))
    block_size = search_block.shape[0]
    kept_local = kept_basis.shape[0]
    slab_sites = search_block.shape[4] * search_block.shape[5]
    norm_scale = 1.0 / (24.0 * slab_sites * time_count)
    applied_re = applied[:, 0].reshape(block_size, 12, slab_sites)
    applied_im = applied[:, 1].reshape(block_size, 12, slab_sites)
    basis_re = kept_basis[:, 0].reshape(kept_local, 12, slab_sites)
    basis_im = kept_basis[:, 1].reshape(kept_local, 12, slab_sites)
    group_size = lax.axis_size("ba")
    group_place = lax.axis_index("ba")
    out_vectors = block_size // group_size
    part_re, part_im = inner_product(basis_re, basis_im, applied_re, applied_im, norm_scale)
    over_mine_re, over_mine_im = (of_everyone(part_re, "ta"), of_everyone(part_im, "ta"))
    proj_re, proj_im = combine_basis(over_mine_re, over_mine_im, basis_re, basis_im)
    full_re, full_im = lax.psum((proj_re, proj_im), "ba")
    rest_re = applied_re - full_re
    rest_im = applied_im - full_im
    gram_part_re, gram_part_im = inner_product(rest_re, rest_im, rest_re, rest_im, norm_scale)
    gram_re, gram_im = (of_everyone(gram_part_re, "ta"), of_everyone(gram_part_im, "ta"))
    lower_re, lower_im = cholesky_complex(gram_re, gram_im)
    inverse_re, inverse_im = invert_lower(lower_re, lower_im)
    own_start = group_place * out_vectors
    coef_re = lax.dynamic_slice_in_dim(inverse_re, own_start, out_vectors, 0).T
    coef_im = -lax.dynamic_slice_in_dim(inverse_im, own_start, out_vectors, 0).T
    back_re, back_im = combine_basis(coef_re, coef_im, rest_re, rest_im)
    ortho_out = jnp.stack([back_re, back_im], 1).reshape(
        out_vectors, 2, 4, 3, search_block.shape[4], search_block.shape[5]
    )
    return (ortho_out, jnp.stack([over_mine_re, over_mine_im], 0))


def solution(mesh):
    placed = (
        P(None, None, None, None, "ta", None),
        P("ba", None, None, None, "ta", None),
        P(None, None, None, None, "ta", None),
        P(None, None, None, None, "ta", None),
    )
    return jax.shard_map(
        per_device,
        mesh=mesh,
        in_specs=placed,
        out_specs=(P("ba", None, None, None, "ta", None), P(None, "ba", None)),
        check_vma=False,
    )
```

profile of v0, /device:TPU:0, one launch (start us, length us, event | category | flops | bytes accessed | tf_op | source)
XLA Modules:
  0.0 413.0 jit_solution(16887749074196854018)
XLA Ops:
  11.1 3.5 collective-permute-start
  36.7 2.3 convolution_bitcast_fusion.4
  39.0 2.4 fusion.25
  41.6 2.3 fusion.191
  44.0 2.7 fusion.188
  59.7 2.4 convolution_bitcast_fusion.5
  62.1 2.4 convolution_bitcast_fusion.6
  64.5 3.5 fusion.192
  72.1 2.5 fusion.51
  96.3 4.0 maximum_subtract_fusion
  102.5 2.5 fusion.6
  105.6 2.5 fusion.3
  108.1 2.7 fusion.2
  129.9 2.5 fusion
  136.7 4.1 collective-permute-start.2
  165.9 4.0 maximum_subtract_fusion.2
  177.7 3.5 all-to-all-start.1
  184.0 3.3 all-to-all-done.1
  187.2 3.5 all-to-all-start
  217.0 86.4 %all-reduce.7.cloned.1.call-done = (f32[16,12,1024]{2,0,1:T(8,128)}, f32[16,12,1024]{2,0,1:T(8,128)}) async-done(((f32[16,12,1024]{2,0,1:T(8,128)}, f32[16,12,1024]{2,0,1:T(8,128)}), (f32[16,12,1024]{2,0,1:T(8,128)}, f32[16,12,1024]{2,0,1:T(8,128)})) %all-reduce.7.cloned.1.call-update) | async-done | bytes 1572880 | tf_op jit(solution)/shard_map/psum | solution.py:227
  309.1 4.6 %all-to-all-start.2 = ((f32[16,1,256]{2,1,0:T(1,128)}), f32[16,1,256]{2,1,0:T(1,128)S(1)}, u32[]{:S(2)}, u32[]{:S(2)}) async-start(f32[16,1,256]{2,1,0:T(1,128)} %reshape.2207), calls=%async_computation.2 | async-start | bytes 32768 | tf_op jit(solution)/shard_map/all_to_all | solution.py:22
  315.6 4.2 %all-to-all-done.2 = f32[16,1,256]{2,1,0:T(1,128)S(1)} async-done(((f32[16,1,256]{2,1,0:T(1,128)}), f32[16,1,256]{2,1,0:T(1,128)S(1)}, u32[]{:S(2)}, u32[]{:S(2)}) %all-to-all-start.2) | async-done | bytes 16416 | tf_op jit(solution)/shard_map/all_to_all | solution.py:22
  319.8 3.5 all-to-all-start.3
  326.4 2.9 all-to-all-done.3
  (638 shorter events, 225.2 us)
Async XLA Ops:
  9.9 4.7 %copy-start.24 = (f32[4,2,3,3,2,512]{5,4,3,2,1,0:T(2,128)S(1)}, f32[4,2,3,3,2,512]{5,4,3,2,1,0:T(2,128)}, u32[]{:S(2)}) copy-start(f32[4,2,3,3,2,512]{5,4,3,2,1,0:T(2,128)} %param.140) | copy-start | bytes 884740
  11.1 79.2 %collective-permute-start = (f32[16,2,2,3,1,512]{5,2,4,3,0,1:T(2,128)}, f32[16,2,2,3,1,512]{5,2,4,3,0,1:T(2,128)}, u32[]{:S(2)}, u32[]{:S(2)}) collective-permute-start(f32[16,2,2,3,1,512]{5,2,4,3,0,1:T(2,128)} %get-tuple-element.984), channel_id=1, source_target_pairs={{0,120},{8,0},{16,8},{24,16},{32,24},{40,32},{48,40},{56,48},{64,5... | collective-permute-start | bytes 1179656 | tf_op jit(solution)/shard_map/ppermute | solution.py:17
  15.3 18.8 %copy-start.32 = (f32[3,3,2,512]{3,2,1,0:T(2,128)}, f32[3,3,2,512]{3,2,1,0:T(2,128)S(1)}, u32[]{:S(2)}) copy-start(f32[3,3,2,512]{3,2,1,0:T(2,128)S(1)} %get-tuple-element.994) | copy-start | bytes 110596
  15.3 18.8 %copy-start.34 = (f32[3,3,2,512]{3,2,1,0:T(2,128)}, f32[3,3,2,512]{3,2,1,0:T(2,128)S(1)}, u32[]{:S(2)}) copy-start(f32[3,3,2,512]{3,2,1,0:T(2,128)S(1)} %get-tuple-element.995) | copy-start | bytes 110596
  15.3 41.5 %copy-start.36 = (f32[3,3,2,512]{3,2,1,0:T(2,128)}, f32[3,3,2,512]{3,2,1,0:T(2,128)S(1)}, u32[]{:S(2)}) copy-start(f32[3,3,2,512]{3,2,1,0:T(2,128)S(1)} %get-tuple-element.996) | copy-start | bytes 110596
  15.3 41.5 %copy-start.38 = (f32[3,3,2,512]{3,2,1,0:T(2,128)}, f32[3,3,2,512]{3,2,1,0:T(2,128)S(1)}, u32[]{:S(2)}) copy-start(f32[3,3,2,512]{3,2,1,0:T(2,128)S(1)} %get-tuple-element.997) | copy-start | bytes 110596
  18.0 75.2 %collective-permute-start.1 = (f32[16,2,2,3,1,512]{5,2,4,3,0,1:T(2,128)}, f32[16,2,2,3,1,512]{5,2,4,3,0,1:T(2,128)}, u32[]{:S(2)}, u32[]{:S(2)}) collective-permute-start(f32[16,2,2,3,1,512]{5,2,4,3,0,1:T(2,128)} %fusion.65), channel_id=1, source_target_pairs={{0,8},{8,16},{16,24},{24,32},{32,40},{40,48},{48,56},{56,64},{64,7... | collective-permute-start | bytes 1179656 | tf_op jit(solution)/shard_map/ppermute | solution.py:17
  24.8 6.8 %copy-start.53 = (pred[512]{0:T(512)(128)(4,1)}, pred[512]{0:T(512)(128)(4,1)S(1)}, u32[]{:S(2)}) copy-start(pred[512]{0:T(512)(128)(4,1)S(1)} %fusion.135) | copy-start | bytes 1540
  25.0 3.6 copy-start.42
  25.0 3.6 copy-start.44
  47.8 6.6 %copy-start.55 = (pred[512]{0:T(512)(128)(4,1)}, pred[512]{0:T(512)(128)(4,1)S(1)}, u32[]{:S(2)}) copy-start(pred[512]{0:T(512)(128)(4,1)S(1)} %broadcast_compare_fusion.1) | copy-start | bytes 1540
  48.0 3.6 copy-start.46
  48.0 3.6 copy-start.48
  52.8 6.0 %copy-start.5 = (f32[16,4,3,2,512]{4,1,3,2,0:T(4,128)}, f32[16,4,3,2,512]{4,1,3,2,0:T(4,128)S(1)}, u32[]{:S(2)}) copy-start(f32[16,4,3,2,512]{4,1,3,2,0:T(4,128)S(1)} %copy.516) | copy-start | bytes 2359300
  53.3 5.4 %copy-start.7 = (f32[16,4,3,2,512]{4,1,3,2,0:T(4,128)}, f32[16,4,3,2,512]{4,1,3,2,0:T(4,128)S(1)}, u32[]{:S(2)}) copy-start(f32[16,4,3,2,512]{4,1,3,2,0:T(4,128)S(1)} %copy.517) | copy-start | bytes 2359300
  91.9 3.4 copy-start.18
  92.2 3.1 copy-start.17
  136.4 28.7 %collective-permute-start.3 = (f32[16,2,2,3,1,512]{5,2,4,3,0,1:T(2,128)S(1)}, f32[16,2,2,3,1,512]{5,2,4,3,0,1:T(2,128)S(1)}, u32[]{:S(2)}, u32[]{:S(2)}) collective-permute-start(f32[16,2,2,3,1,512]{5,2,4,3,0,1:T(2,128)S(1)} %fusion.62), channel_id=1, source_target_pairs={{0,8},{8,16},{16,24},{24,32},{32,40},{40,48},{48,56},{56,64},{64,7... | collective-permute-start | bytes 1179656 | tf_op jit(solution)/shard_map/ppermute | solution.py:17
  136.7 26.2 %collective-permute-start.2 = (f32[16,2,2,3,1,512]{5,2,4,3,0,1:T(2,128)S(1)}, f32[16,2,2,3,1,512]{5,2,4,3,0,1:T(2,128)S(1)}, u32[]{:S(2)}, u32[]{:S(2)}) collective-permute-start(f32[16,2,2,3,1,512]{5,2,4,3,0,1:T(2,128)S(1)} %get-tuple-element.974), channel_id=1, source_target_pairs={{0,120},{8,0},{16,8},{24,16},{32,24},{40,32},{48,40},{56,48},{64,5... | collective-permute-start | bytes 1179656 | tf_op jit(solution)/shard_map/ppermute | solution.py:17
  177.7 9.5 %all-to-all-start.1 = ((f32[16,1,256]{2,1,0:T(1,128)}), f32[16,1,256]{2,1,0:T(1,128)S(1)}, u32[]{:S(2)}, u32[]{:S(2)}) async-start(f32[16,1,256]{2,1,0:T(1,128)} %reshape.2205), calls=%async_computation.1 | async-start | bytes 32768 | tf_op jit(solution)/shard_map/all_to_all | solution.py:22
  187.2 11.0 %all-to-all-start = ((f32[16,1,256]{2,1,0:T(1,128)}), f32[16,1,256]{2,1,0:T(1,128)S(1)}, u32[]{:S(2)}, u32[]{:S(2)}) async-start(f32[16,1,256]{2,1,0:T(1,128)} %reshape.2203), calls=%async_computation | async-start | bytes 32768 | tf_op jit(solution)/shard_map/all_to_all | solution.py:22
  190.7 112.7 %all-reduce.7.cloned.1.call-start = ((), (), s32[]{:S(2)}) async-start(), calls=%async_computation.4 | async-start | bytes 3145728 | tf_op jit(solution)/shard_map/psum | solution.py:227
  309.1 10.7 %all-to-all-start.2 = ((f32[16,1,256]{2,1,0:T(1,128)}), f32[16,1,256]{2,1,0:T(1,128)S(1)}, u32[]{:S(2)}, u32[]{:S(2)}) async-start(f32[16,1,256]{2,1,0:T(1,128)} %reshape.2207), calls=%async_computation.2 | async-start | bytes 32768 | tf_op jit(solution)/shard_map/all_to_all | solution.py:22
  319.8 9.5 %all-to-all-start.3 = ((f32[16,1,256]{2,1,0:T(1,128)}), f32[16,1,256]{2,1,0:T(1,128)S(1)}, u32[]{:S(2)}, u32[]{:S(2)}) async-start(f32[16,1,256]{2,1,0:T(1,128)} %reshape.2209), calls=%async_computation.3 | async-start | bytes 32768 | tf_op jit(solution)/shard_map/all_to_all | solution.py:22
  (42 other events, 58.7 us)
Sparse Core Ops, SparseCore 0:
  204.3 99.0 all-reduce.6
where the time goes:
time: 419 us; the launch traced here: 413 us
  other arithmetic  126 us (30%)
  local copies, waits for them, and re-layouts  97 us (23%)
  waiting for transfers between devices  96.9 us (23%)
  matrix products  40.6 us (10%)
  between operations  29.6 us (7%)
  starting transfers between devices  23.1 us (6%)
    psum x1, waiting for transfers between devices, per_device(): full_re, full_im = lax.psum((proj_re, proj_im), 'ba')  86.4 us
    another operation x44, other arithmetic  29.9 us
    concatenate x11, other arithmetic, gamma_five(): return jnp.concatenate([spinor[:, :, :2], -spinor[:, :, 2:]], axis=2)  15.5 us
    mul x42, local copies, waits for them, and re-layouts, colour(): out_re = jnp.sum(link_re * field_re - link_im * field_im, axis=3)  15.3 us
    all_to_all x4, starting transfers between devices, from_everyone(): lax.all_to_all(jnp.broadcast_to(value[None], (count, *value.shape)), axis...  15.1 us
    reduce_sum x15, other arithmetic, colour(): out_re = jnp.sum(link_re * field_re - link_im * field_im, axis=3)  11.1 us
    div x16, other arithmetic, invert_lower(): inverse_re = inverse_re.at[row_index].set((unit_row - sum_re) / pivot_value)  10.7 us
    dot_general x6, matrix products, gamma_apply(): jnp.einsum('as,vsctx->vactx', matrix, field_im, precision=HIGHEST)  10.6 us
  transfers between devices with their start and end apart: 9, of which 4 were waited for; matrix products, arithmetic and copies ran while one was open for 31% of the time, Pallas kernels for 0%

commit v1 on v0

v1 whole, which is shorter than its diff:
```python
import jax
import jax.numpy as jnp
from jax import lax
from jax.experimental import pallas as pl
from jax.experimental.pallas import tpu as pltpu
from jax.sharding import PartitionSpec as P

MESH = pl.DeviceIdType.MESH
F32 = jnp.float32
BF16 = jnp.bfloat16

HOPPING = 0.13
NTA, NBA = 16, 8
BLOCK = 16
KEPT = 128
GROUP = KEPT // NBA
MINE = BLOCK // NBA
COMPS = 24
PLANES = 12
LANES = 128
WIDE = PLANES * LANES

ISIGMA = (
    ((1, True, 1), (0, True, 1)),
    ((1, False, 1), (0, False, -1)),
    ((0, True, 1), (1, True, -1)),
)

NT_DIMS = (((1,), (1,)), ((), ()))
NN_DIMS = (((1,), (0,)), ((), ()))


def split(value):
    high = value.astype(BF16)
    return high, (value - high.astype(F32)).astype(BF16)


def matmul(left, right, dims):
    return lax.dot_general(left, right, dims, preferred_element_type=F32)


def comp(ri, spin, colour):
    return ri * 12 + spin * 3 + colour


def half(ri, spin, colour):
    return ri * 6 + spin * 3 + colour


def add_phase(base, other, imag, sign):
    if imag:
        other = (other[1], other[0])
        signs = (-sign, sign)
    else:
        signs = (sign, sign)
    return tuple(b + o if s > 0 else b - o for b, o, s in zip(base, other, signs))


def kernel(
    search, basis, links, clover, out, corr,
    psi, lk, cl, acc, h_t, b_t, dn, up, rdn, rup,
    basis_all, b_hi, b_lo, a_all, xf, x_hi, x_lo, cm, c_part, c_ba, c_sum, c_ta, c_full,
    wm, r_hi, r_lo, g_part, g_ta, g_sum, g_ba, vm, osend,
    in_sem, hs, hr, bs, br, as_, ar, cs1, cr1, cs2, cr2, gs1, gr1, gs2, gr2, os_, or_,
):
    ta = lax.axis_index("ta")
    ba = lax.axis_index("ba")
    above = (lax.rem(ta + 1, NTA), ba)
    below = (lax.rem(ta + NTA - 1, NTA), ba)

    def ta_peer(k):
        return lax.rem(ta + k, NTA)

    def ba_peer(k):
        return lax.rem(ba + k, NBA)

    barrier = pltpu.get_barrier_semaphore()
    for k in range(1, NTA):
        pl.semaphore_signal(barrier, inc=1, device_id=(ta_peer(k), ba), device_id_type=MESH)
    for k in range(1, NBA):
        pl.semaphore_signal(barrier, inc=1, device_id=(ta, ba_peer(k)), device_id_type=MESH)

    own = pl.multiple_of(ba * MINE * COMPS, 8)
    load_psi = pltpu.make_async_copy(
        search.at[pl.ds(own, MINE * COMPS)], psi.at[0], in_sem.at[0]
    )
    load_links = pltpu.make_async_copy(links, lk, in_sem.at[1])
    load_clover = pltpu.make_async_copy(clover, cl, in_sem.at[2])
    load_basis = pltpu.make_async_copy(basis.at[:, ba], basis_all.at[pl.ds(pl.multiple_of(ba * GROUP * COMPS, 8), GROUP * COMPS)], br.at[ba])
    load_psi.start()
    load_links.start()
    load_clover.start()
    load_basis.start()

    lane = lax.broadcasted_iota(jnp.int32, (8, LANES), 1)
    sub = lax.broadcasted_iota(jnp.int32, (8, LANES), 0)
    z_lane = lane % 8
    y_lane = (lane // 8) % 8
    z_last, z_first = z_lane == 7, z_lane == 0
    y_last, y_first = y_lane == 7, y_lane == 0
    x_even = lane < 64
    t_odd = sub % 2 == 1
    sign_last = jnp.where(ta == NTA - 1, -1.0, 1.0).astype(F32)
    sign_first = jnp.where(ta == 0, -1.0, 1.0).astype(F32)

    def lroll(value, shift):
        return pltpu.roll(value, shift, 1)

    def sroll(value, shift):
        return pltpu.roll(value, shift, 0)

    def ahead(value, mu):
        if mu == 0:
            turned = lroll(value, 64)
            return jnp.where(x_even, turned, sroll(turned, 6))
        if mu == 1:
            return jnp.where(y_last, lroll(value, 56), lroll(value, 120))
        return jnp.where(z_last, lroll(value, 7), lroll(value, 127))

    def behind(value, mu):
        if mu == 0:
            turned = lroll(value, 64)
            return jnp.where(x_even, sroll(turned, 2), turned)
        if mu == 1:
            return jnp.where(y_first, lroll(value, 72), lroll(value, 8))
        return jnp.where(z_first, lroll(value, 121), lroll(value, 1))

    def link(mu, row, col):
        place = mu * 18 + row * 3 + col
        return lk[place], lk[place + 9]

    def times_link(mu, vec):
        result = []
        for row in range(3):
            re = im = None
            for col in range(3):
                ur, ui = link(mu, row, col)
                vr, vi = vec[col]
                tr, ti = ur * vr - ui * vi, ur * vi + ui * vr
                re, im = (tr, ti) if re is None else (re + tr, im + ti)
            result.append((re, im))
        return result

    def times_dagger(mu, vec):
        result = []
        for row in range(3):
            re = im = None
            for col in range(3):
                ur, ui = link(mu, col, row)
                vr, vi = vec[col]
                tr, ti = ur * vr + ui * vi, ur * vi - ui * vr
                re, im = (tr, ti) if re is None else (re + tr, im + ti)
            result.append((re, im))
        return result

    def time_prepare(a):
        def one(v, carry):
            def field(spin, colour):
                base = v * COMPS
                return psi[a, base + comp(0, spin, colour)], psi[a, base + comp(1, spin, colour)]

            for spin in range(2):
                sums = []
                for colour in range(3):
                    upper, lower = field(spin, colour), field(spin + 2, colour)
                    for ri in range(2):
                        h_t[v * 12 + half(ri, spin, colour)] = upper[ri] - lower[ri]
                    sums.append((upper[0] + lower[0], upper[1] + lower[1]))
                linked = times_dagger(3, sums)
                for colour in range(3):
                    for ri in range(2):
                        b_t[v * 12 + half(ri, spin, colour)] = linked[colour][ri]
            return carry

        lax.fori_loop(0, MINE, one, 0)
        for i in range(12):
            dn[a, i] = jnp.where(t_odd, sroll(h_t[12 + i], 1), h_t[i])
            up[a, i] = jnp.where(t_odd, b_t[12 + i], sroll(b_t[i], 7))

    def halo_copies(a):
        down = pltpu.make_async_remote_copy(
            src_ref=dn.at[a], dst_ref=rdn.at[a], send_sem=hs.at[a, 0], recv_sem=hr.at[a, 0],
            device_id=below, device_id_type=MESH,
        )
        upward = pltpu.make_async_remote_copy(
            src_ref=up.at[a], dst_ref=rup.at[a], send_sem=hs.at[a, 1], recv_sem=hr.at[a, 1],
            device_id=above, device_id_type=MESH,
        )
        return down, upward

    def local_part(a):
        def one(v, carry):
            base = v * COMPS

            def field(spin, colour):
                return psi[a, base + comp(0, spin, colour)], psi[a, base + comp(1, spin, colour)]

            for chiral in range(2):
                vec = [field(2 * chiral + i // 3, i % 3) for i in range(6)]
                for row in range(6):
                    re = im = None
                    for col in range(6):
                        place = chiral * 72 + row * 6 + col
                        cr, ci = cl[place], cl[place + 36]
                        vr, vi = vec[col]
                        tr, ti = cr * vr - ci * vi, cr * vi + ci * vr
                        re, im = (tr, ti) if re is None else (re + tr, im + ti)
                    spin = 2 * chiral + row // 3
                    acc[base + comp(0, spin, row % 3)] = re
                    acc[base + comp(1, spin, row % 3)] = im
            for mu in range(3):
                for spin in range(2):
                    source, imag, sign = ISIGMA[mu][spin]
                    forward, backward = [], []
                    for colour in range(3):
                        upper, lower = field(spin, colour), field(2 + source, colour)
                        minus = add_phase(upper, lower, imag, sign)
                        plus = add_phase(upper, lower, imag, -sign)
                        forward.append(tuple(ahead(value, mu) for value in minus))
                        backward.append(plus)
                    forward = times_link(mu, forward)
                    backward = times_dagger(mu, backward)
                    backward = [tuple(behind(value, mu) for value in pair) for pair in backward]
                    target = [s for s in range(2) if ISIGMA[mu][s][0] == spin][0]
                    _, imag, sign = ISIGMA[mu][target]
                    for colour in range(3):
                        f, b = forward[colour], backward[colour]
                        for ri in range(2):
                            place = base + comp(ri, spin, colour)
                            acc[place] = acc[place] + (f[ri] + b[ri])
                        places = [base + comp(ri, 2 + target, colour) for ri in range(2)]
                        total = add_phase(
                            (acc[places[0]], acc[places[1]]), (b[0] - f[0], b[1] - f[1]), imag, sign
                        )
                        acc[places[0]] = total[0]
                        acc[places[1]] = total[1]
            return carry

        lax.fori_loop(0, MINE, one, 0)

    def time_finish(a):
        for v in range(MINE):
            for spin in range(2):
                front, back = [], []
                for colour in range(3):
                    f, b = [], []
                    for ri in range(2):
                        i = half(ri, spin, colour)
                        got, low = rdn[a, i] * sign_last, rup[a, i] * sign_first
                        got = sroll(got, 1) if v == 0 else got
                        low = low if v == 0 else sroll(low, 7)
                        f.append(jnp.where(t_odd, got, sroll(h_t[v * 12 + i], 7)))
                        b.append(jnp.where(t_odd, sroll(b_t[v * 12 + i], 1), low))
                    front.append(tuple(f))
                    back.append(tuple(b))
                front = times_link(3, front)
                for colour in range(3):
                    for ri in range(2):
                        f, b = front[colour][ri], back[colour][ri]
                        upper = v * COMPS + comp(ri, spin, colour)
                        lower = v * COMPS + comp(ri, spin + 2, colour)
                        psi[a + 1, upper] = acc[upper] + (f + b)
                        psi[a + 1, lower] = (f - b) - acc[lower]

    load_psi.wait()
    load_links.wait()

    def scale_link(i, carry):
        lk[i] = lk[i] * (-HOPPING)
        return carry

    lax.fori_loop(0, 72, scale_link, 0)
    time_prepare(0)
    load_clover.wait()

    pl.semaphore_wait(barrier, NTA + NBA - 2)

    first_halo = halo_copies(0)
    for copy in first_halo:
        copy.start()

    def block_of(ref, place, size):
        return ref.at[pl.ds(pl.multiple_of(place * size, 8), size)]

    basis_sends = [
        pltpu.make_async_remote_copy(
            src_ref=basis.at[:, ba_peer(k)], dst_ref=block_of(basis_all, ba, GROUP * COMPS),
            send_sem=bs.at[k], recv_sem=br.at[ba],
            device_id=(ta, ba_peer(k)), device_id_type=MESH,
        )
        for k in range(1, NBA)
    ]
    for copy in basis_sends:
        copy.start()

    local_part(0)
    for copy in first_halo:
        copy.wait_recv()
    time_finish(0)
    time_prepare(1)
    second_halo = halo_copies(1)
    for copy in second_halo:
        copy.start()
    local_part(1)
    for copy in second_halo:
        copy.wait_recv()
    time_finish(1)

    applied_sends = [
        pltpu.make_async_remote_copy(
            src_ref=psi.at[2, :, ba_peer(k)], dst_ref=block_of(a_all, ba, MINE * COMPS),
            send_sem=as_.at[k], recv_sem=ar.at[ba],
            device_id=(ta, ba_peer(k)), device_id_type=MESH,
        )
        for k in range(1, NBA)
    ]
    for copy in applied_sends:
        copy.start()
    pltpu.make_async_copy(psi.at[2, :, ba], block_of(a_all, ba, MINE * COMPS), ar.at[ba]).start()
    cm[...] = jnp.zeros_like(cm)
    for k in range(NBA):
        place = block_of(a_all, ba_peer(k), MINE * COMPS)
        pltpu.make_async_copy(place, place, ar.at[ba_peer(k)]).wait()

    for plane in range(PLANES):
        columns = slice(plane * LANES, (plane + 1) * LANES)
        later = slice(WIDE + plane * LANES, WIDE + (plane + 1) * LANES)
        re = a_all[pl.ds(plane, BLOCK, stride=COMPS), :]
        im = a_all[pl.ds(PLANES + plane, BLOCK, stride=COMPS), :]
        xf[0:BLOCK, columns] = re
        xf[BLOCK : 2 * BLOCK, columns] = im
        (re_hi, re_lo), (im_hi, im_lo) = split(re), split(im)
        x_hi[0:BLOCK, columns] = re_hi
        x_hi[BLOCK : 2 * BLOCK, columns] = im_hi
        x_hi[0:BLOCK, later] = im_hi
        x_hi[BLOCK : 2 * BLOCK, later] = -re_hi
        x_lo[0:BLOCK, columns] = re_lo
        x_lo[BLOCK : 2 * BLOCK, columns] = im_lo
        x_lo[0:BLOCK, later] = im_lo
        x_lo[BLOCK : 2 * BLOCK, later] = -re_lo

    def basis_chunk(k, carry):
        source = lax.rem(ba + k, NBA)
        place = block_of(basis_all, source, GROUP * COMPS)
        pltpu.make_async_copy(place, place, br.at[source]).wait()
        highs, lows = [], []
        for c in range(COMPS):
            part = basis_all[pl.ds(source * (GROUP * COMPS) + c, GROUP, stride=COMPS), :]
            hi, lo = split(part)
            highs.append(hi)
            lows.append(lo)
            rows = pl.ds(pl.multiple_of((c // PLANES) * KEPT + source * GROUP, GROUP), GROUP)
            columns = slice((c % PLANES) * LANES, (c % PLANES + 1) * LANES)
            b_hi[rows, columns] = hi
            b_lo[rows, columns] = lo
        high = jnp.concatenate(highs, axis=1)
        low = jnp.concatenate(lows, axis=1)
        both = matmul(jnp.concatenate([high, low], axis=0), x_hi[...], NT_DIMS)
        total = both[0:GROUP] + both[GROUP : 2 * GROUP] + matmul(high, x_lo[...], NT_DIMS)
        cm[pl.ds(pl.multiple_of(source * GROUP, GROUP), GROUP), 0 : 2 * BLOCK] = total
        return carry

    lax.fori_loop(0, NBA, basis_chunk, 0)

    c_part[...] = cm[...].T[0 : 2 * BLOCK]
    corr_sends = [
        pltpu.make_async_remote_copy(
            src_ref=c_part, dst_ref=c_ba.at[ba], send_sem=cs1.at[k], recv_sem=cr1.at[ba],
            device_id=(ta, ba_peer(k)), device_id_type=MESH,
        )
        for k in range(1, NBA)
    ]
    for copy in corr_sends:
        copy.start()
    c_ba[ba] = c_part[...]
    for k in range(1, NBA):
        pltpu.make_async_copy(c_ba.at[ba_peer(k)], c_ba.at[ba_peer(k)], cr1.at[ba_peer(k)]).wait()
    total = c_ba[0]
    for k in range(1, NBA):
        total = total + c_ba[k]
    c_sum[...] = total
    more_sends = [
        pltpu.make_async_remote_copy(
            src_ref=c_sum, dst_ref=c_ta.at[ta], send_sem=cs2.at[k], recv_sem=cr2.at[ta],
            device_id=(ta_peer(k), ba), device_id_type=MESH,
        )
        for k in range(1, NTA)
    ]
    for copy in more_sends:
        copy.start()
    c_ta[ta] = c_sum[...]
    for k in range(1, NTA):
        pltpu.make_async_copy(c_ta.at[ta_peer(k)], c_ta.at[ta_peer(k)], cr2.at[ta_peer(k)]).wait()
    total = c_ta[0]
    for k in range(1, NTA):
        total = total + c_ta[k]
    norm = 1.0 / (24.0 * 512 * 2 * NTA)
    total = total * norm
    c_full[0 : 2 * BLOCK] = total
    c_re, c_im = split(total[0:BLOCK]), split(total[BLOCK : 2 * BLOCK])
    for level in range(2):
        rows = level * 2 * BLOCK
        wm[rows : rows + BLOCK, 0:KEPT] = c_re[level]
        wm[rows + BLOCK : rows + 2 * BLOCK, 0:KEPT] = c_im[level]
        wm[rows : rows + BLOCK, KEPT : 2 * KEPT] = -c_im[level]
        wm[rows + BLOCK : rows + 2 * BLOCK, KEPT : 2 * KEPT] = c_re[level]

    step = 2 * LANES
    for start in range(0, WIDE, step):
        columns = slice(start, start + step)
        both = matmul(wm[...], b_hi[:, columns], NN_DIMS)
        low = matmul(wm[0 : 2 * BLOCK], b_lo[:, columns], NN_DIMS)
        rest = xf[:, columns] - (both[0 : 2 * BLOCK] + both[2 * BLOCK : 4 * BLOCK] + low)
        hi, lo = split(rest)
        r_hi[:, columns] = hi
        r_lo[:, columns] = lo

    both = matmul(jnp.concatenate([r_hi[...], r_lo[...]], axis=0), r_hi[...], NT_DIMS)
    gram = both[0 : 2 * BLOCK] + both[2 * BLOCK : 4 * BLOCK]
    gram = gram + matmul(r_hi[...], r_lo[...], NT_DIMS)
    vm[...] = jnp.zeros_like(vm)
    vm[:, 0 : 2 * BLOCK] = gram
    lane16 = lax.broadcasted_iota(jnp.int32, (BLOCK, LANES), 1)
    row16 = lax.broadcasted_iota(jnp.int32, (BLOCK, LANES), 0)
    upper, lower = vm[0:BLOCK], vm[BLOCK : 2 * BLOCK]
    turned = jnp.where(lane16 < BLOCK, lroll(lower, LANES - BLOCK), -lroll(lower, BLOCK))
    both = upper + turned
    g_part[...] = jnp.where(lane < 32, both[0:8], lroll(both[8:16], 32))

    gram_sends = [
        pltpu.make_async_remote_copy(
            src_ref=g_part, dst_ref=g_ta.at[ta], send_sem=gs1.at[k], recv_sem=gr1.at[ta],
            device_id=(ta_peer(k), ba), device_id_type=MESH,
        )
        for k in range(1, NTA)
    ]
    for copy in gram_sends:
        copy.start()
    g_ta[ta] = g_part[...]
    c_full[2 * BLOCK : LANES] = jnp.zeros((LANES - 2 * BLOCK, KEPT), F32)
    cm[...] = c_full[...].T
    mine = pl.ds(pl.multiple_of(ba * GROUP, GROUP), GROUP)
    corr[0] = cm[mine, 0:BLOCK]
    corr[1] = cm[mine, BLOCK : 2 * BLOCK]
    for k in range(1, NTA):
        pltpu.make_async_copy(g_ta.at[ta_peer(k)], g_ta.at[ta_peer(k)], gr1.at[ta_peer(k)]).wait()
    total = g_ta[0]
    for k in range(1, NTA):
        total = total + g_ta[k]
    g_sum[...] = total
    gram_more = [
        pltpu.make_async_remote_copy(
            src_ref=g_sum, dst_ref=g_ba.at[ba], send_sem=gs2.at[k], recv_sem=gr2.at[ba],
            device_id=(ta, ba_peer(k)), device_id_type=MESH,
        )
        for k in range(1, NBA)
    ]
    for copy in gram_more:
        copy.start()
    g_ba[ba] = g_sum[...]
    for k in range(1, NBA):
        pltpu.make_async_copy(g_ba.at[ba_peer(k)], g_ba.at[ba_peer(k)], gr2.at[ba_peer(k)]).wait()
    total = g_ba[0]
    for k in range(1, NBA):
        total = total + g_ba[k]
    total = total * norm

    gram = jnp.concatenate([total, lroll(total, LANES - 32)], axis=0)
    m_re = jnp.where(lane16 < BLOCK, gram, jnp.where(lane16 == row16 + BLOCK, 1.0, 0.0))
    m_im = jnp.where(lane16 < BLOCK, lroll(gram, LANES - BLOCK), 0.0)
    for c in range(BLOCK):
        scale = lax.rsqrt(m_re[c : c + 1, c : c + 1])
        row_re = m_re[c : c + 1, :] * scale
        row_im = m_im[c : c + 1, :] * scale
        f_re = m_re[:, c : c + 1] * scale
        f_im = m_im[:, c : c + 1] * scale
        below_row = row16 > c
        at_row = row16 == c
        new_re = m_re - (f_re * row_re - f_im * row_im)
        new_im = m_im - (f_re * row_im + f_im * row_re)
        m_re = jnp.where(below_row, new_re, jnp.where(at_row, row_re, m_re))
        m_im = jnp.where(below_row, new_im, jnp.where(at_row, row_im, m_im))

    vm[0:BLOCK] = jnp.where(lane16 < BLOCK, lroll(m_re, LANES - BLOCK), m_im)
    vm[BLOCK : 2 * BLOCK] = jnp.where(lane16 < BLOCK, -lroll(m_im, LANES - BLOCK), m_re)
    v_hi, v_lo = split(vm[:, 0 : 2 * BLOCK])
    v_both = jnp.concatenate([v_hi, v_lo], axis=0)
    for start in range(0, WIDE, step):
        columns = slice(start, start + step)
        both = matmul(v_both, r_hi[:, columns], NN_DIMS)
        low = matmul(v_hi, r_lo[:, columns], NN_DIMS)
        ortho = both[0 : 2 * BLOCK] + both[2 * BLOCK : 4 * BLOCK] + low
        for offset in range(0, step, LANES):
            plane = (start + offset) // LANES
            for ri in range(2):
                part = ortho[ri * BLOCK : (ri + 1) * BLOCK, offset : offset + LANES]
                osend[pl.ds(ri * PLANES + plane, BLOCK, stride=COMPS), :] = part

    out_sends = [
        pltpu.make_async_remote_copy(
            src_ref=block_of(osend, ba_peer(k), MINE * COMPS), dst_ref=out.at[:, ba],
            send_sem=os_.at[k], recv_sem=or_.at[ba],
            device_id=(ta, ba_peer(k)), device_id_type=MESH,
        )
        for k in range(1, NBA)
    ]
    for copy in out_sends:
        copy.start()
    pltpu.make_async_copy(block_of(osend, ba, MINE * COMPS), out.at[:, ba], or_.at[ba]).start()
    for copy in (*first_halo, *second_halo, *basis_sends, *applied_sends, *corr_sends, *more_sends):
        copy.wait_send()
    for copy in (*gram_sends, *gram_more, *out_sends):
        copy.wait_send()
    for k in range(NBA):
        place = block_of(osend, ba_peer(k), MINE * COMPS)
        pltpu.make_async_copy(place, out.at[:, ba_peer(k)], or_.at[ba_peer(k)]).wait()


def tiles(array):
    times, sites = array.shape[-2:]
    split_up = array.reshape(*array.shape[:-1], sites // LANES, LANES)
    return jnp.swapaxes(split_up, -3, -2).reshape(-1, times * (sites // LANES), LANES)


def untiles(array, shape):
    *lead, times, sites = shape
    split_up = array.reshape(*lead, sites // LANES, times, LANES)
    return jnp.swapaxes(split_up, -3, -2).reshape(shape)


def per_device(search_block, kept_basis, gauge_links, clover_term):
    anywhere = pl.BlockSpec(memory_space=pl.ANY)
    in_vmem = pl.BlockSpec(memory_space=pltpu.VMEM)
    dma = pltpu.SemaphoreType.DMA
    vmem = pltpu.VMEM
    two = 2 * BLOCK
    scratch = [
        vmem((3, MINE * COMPS, 8, LANES), F32),
        vmem((72, 8, LANES), F32),
        vmem((144, 8, LANES), F32),
        vmem((MINE * COMPS, 8, LANES), F32),
        vmem((MINE * 12, 8, LANES), F32),
        vmem((MINE * 12, 8, LANES), F32),
        vmem((2, 12, 8, LANES), F32),
        vmem((2, 12, 8, LANES), F32),
        vmem((2, 12, 8, LANES), F32),
        vmem((2, 12, 8, LANES), F32),
        vmem((KEPT * COMPS, LANES), F32),
        vmem((2 * KEPT, WIDE), BF16),
        vmem((2 * KEPT, WIDE), BF16),
        vmem((BLOCK * COMPS, LANES), F32),
        vmem((two, WIDE), F32),
        vmem((two, 2 * WIDE), BF16),
        vmem((two, 2 * WIDE), BF16),
        vmem((KEPT, LANES), F32),
        vmem((two, KEPT), F32),
        vmem((NBA, two, KEPT), F32),
        vmem((two, KEPT), F32),
        vmem((NTA, two, KEPT), F32),
        vmem((LANES, KEPT), F32),
        vmem((2 * two, 2 * KEPT), BF16),
        vmem((two, WIDE), BF16),
        vmem((two, WIDE), BF16),
        vmem((8, LANES), F32),
        vmem((NTA, 8, LANES), F32),
        vmem((8, LANES), F32),
        vmem((NBA, 8, LANES), F32),
        vmem((two, LANES), F32),
        vmem((BLOCK * COMPS, LANES), F32),
        dma((3,)), dma((2, 2)), dma((2, 2)),
        dma((NBA,)), dma((NBA,)), dma((NBA,)), dma((NBA,)), dma((NBA,)), dma((NBA,)),
        dma((NTA,)), dma((NTA,)), dma((NTA,)), dma((NTA,)),
        dma((NBA,)), dma((NBA,)), dma((NBA,)), dma((NBA,)),
    ]
    ortho, correlations = pl.pallas_call(
        kernel,
        out_shape=(
            jax.ShapeDtypeStruct((MINE * COMPS, 8, LANES), F32),
            jax.ShapeDtypeStruct((2, GROUP, BLOCK), F32),
        ),
        in_specs=[anywhere] * 4,
        out_specs=(in_vmem, in_vmem),
        scratch_shapes=scratch,
        compiler_params=pltpu.CompilerParams(
            collective_id=0, has_side_effects=True, vmem_limit_bytes=56 * 1024 * 1024
        ),
    )(tiles(search_block), tiles(kept_basis), tiles(gauge_links), tiles(clover_term))
    slab = search_block.shape[-2:]
    return untiles(ortho, (MINE, 2, 4, 3, *slab)), correlations


def solution(mesh):
    over_time = P(None, None, None, None, "ta", None)
    grouped = P("ba", None, None, None, "ta", None)
    return jax.shard_map(
        per_device,
        mesh=mesh,
        in_specs=(over_time, grouped, over_time, over_time),
        out_specs=(grouped, P(None, "ba", None)),
        check_vma=False,
    )
```

time: 419 us -> 67.9 us (0.16); the launches traced: 413 us -> 67.7 us
  other arithmetic: 126 us -> 0 us
  waiting for transfers between devices: 96.9 us -> 0 us
  local copies, waits for them, and re-layouts: 97 us -> 2.94 us
  Pallas kernels: 0 us -> 64.2 us
  matrix products: 40.6 us -> 0 us
  between operations: 29.6 us -> 0.64 us
  starting transfers between devices: 23.1 us -> 0 us
    psum x1 -> x0, waiting for transfers between devices: 86.4 us -> none  [per_device(): full_re, full_im = lax.psum((proj_re, proj_im), 'ba')]
    pallas_call x0 -> x1, Pallas kernels: none -> 64.2 us  [per_device(): pl.pallas_call(kernel, out_shape=(jax.ShapeDtypeStruct((MINE * COMPS, 8,...]
    dot_general x28 -> x0, matrix products: 40.6 us -> none  [the longest x6 10.6 us: gamma_apply(): jnp.einsum('as,vsctx->vactx', matrix, field_im, precision=HIGHEST)]
    slice x46 -> x0, local copies, waits for them, and re-layouts: 38.5 us -> none  [the longest x6 10.6 us: shift_space(): jnp.roll(values, (LS - 1) * stride, axis=-1)]
    another operation x48 -> x0, other arithmetic: 31.8 us -> none
    div x31 -> x0, other arithmetic: 20.1 us -> none  [the longest x16 10.7 us: invert_lower(): inverse_re = inverse_re.at[row_index].set((unit_row - sum_re) / pivot_value)]
    reduce_sum x52 -> x0, other arithmetic: 16.9 us -> none  [the longest x15 11.1 us: colour(): out_re = jnp.sum(link_re * field_re - link_im * field_im, axis=3)]
    mul x80 -> x0, local copies, waits for them, and re-layouts: 16.1 us -> none  [the longest x42 15.3 us: colour(): out_re = jnp.sum(link_re * field_re - link_im * field_im, axis=3)]
  transfers between devices with their start and end apart: 9 -> 0, of which waited for: 4 -> 0; matrix products, arithmetic and copies ran while one was open for 31% -> 0% of each run, Pallas kernels for 0% -> 0%
where the time goes in v1:
time: 67.9 us; the launch traced here: 67.7 us
  Pallas kernels  64.2 us (95%)
  local copies, waits for them, and re-layouts  2.94 us (4%)
    pallas_call x1, Pallas kernels, per_device(): pl.pallas_call(kernel, out_shape=(jax.ShapeDtypeStruct((MINE * COMPS, 8,...  64.2 us
    unnamed x2, local copies, waits for them, and re-layouts  2.94 us

profile of v1, /device:TPU:0, one launch (start us, length us, event | category | flops | bytes accessed | tf_op | source)
XLA Modules:
  0.0 67.7 jit_solution(15196683671383799939)
XLA Ops:
  0.6 64.2 %shard_map.59 = (f32[48,8,128]{2,1,0:T(8,128)}, f32[2,16,16]{2,1,0:T(8,128)}) custom-call(f32[384,8,128]{2,1,0:T(8,128)} %bitcast.25, f32[384,8,128]{2,1,0:T(8,128)} %bitcast.26, f32[72,8,128]{2,1,0:T(8,128)} %bitcast.28, f32[144,8,128]{2,1,0:T(8,128)} %bitcast.27), custom_call_target="tpu_custom_call" | custom-call | tf_op jit(solution)/shard_map/pallas_call | solution.py:575
  64.8 1.6 %copy.13 = f32[2,2,4,3,2,512]{5,4,3,2,1,0:T(2,128)} copy(f32[2,2,4,3,2,512]{5,4,3,2,1,0:T(2,128)} %bitcast.29) | data formatting | bytes 393216
  66.4 1.3 %copy.14 = f32[2,16,16]{2,1,0:T(8,128)} copy(f32[2,16,16]{2,1,0:T(8,128)} %get-tuple-element.9) | data formatting | bytes 4096

commit v2 on v1

--- a/solution.py
+++ b/solution.py
@@ -20,6 +20,13 @@
 LANES = 128
 WIDE = PLANES * LANES
 
+PIECES = 2
+ORDER = (
+    ((1, 0), (0, 1), (3, 0), (1, 1), (2, 0), (3, 1), (2, 1)),
+    ((0, 1), (3, 0), (1, 1), (1, 0), (3, 1), (2, 1), (2, 0)),
+)
+PACE = (3, 0, 4, 0, 7)
+
 ISIGMA = (
     ((1, True, 1), (0, True, 1)),
     ((1, False, 1), (0, False, -1)),
@@ -59,9 +66,9 @@
 def kernel(
     search, basis, links, clover, out, corr,
     psi, lk, cl, acc, h_t, b_t, dn, up, rdn, rup,
-    basis_all, b_hi, b_lo, a_all, xf, x_hi, x_lo, cm, c_part, c_ba, c_sum, c_ta, c_full,
+    basis_all, b_hi, b_lo, a_all, xf, x_hi, x_lo, cm, c_part, c_sum, c_ba, c_ta, c_full,
     wm, r_hi, r_lo, g_part, g_ta, g_sum, g_ba, vm, osend,
-    in_sem, hs, hr, bs, br, as_, ar, cs1, cr1, cs2, cr2, gs1, gr1, gs2, gr2, os_, or_,
+    in_sem, hs, hr, bs, br, as_, ar, cs, cr, gs1, gr1, gs2, gr2, os_, or_,
 ):
     ta = lax.axis_index("ta")
     ba = lax.axis_index("ba")
@@ -272,6 +279,7 @@
     lax.fori_loop(0, 72, scale_link, 0)
     time_prepare(0)
     load_clover.wait()
+    local_part(0)
 
     pl.semaphore_wait(barrier, NTA + NBA - 2)
 
@@ -282,26 +290,38 @@
     def block_of(ref, place, size):
         return ref.at[pl.ds(pl.multiple_of(place * size, 8), size)]
 
-    basis_sends = [
-        pltpu.make_async_remote_copy(
-            src_ref=basis.at[:, ba_peer(k)], dst_ref=block_of(basis_all, ba, GROUP * COMPS),
-            send_sem=bs.at[k], recv_sem=br.at[ba],
-            device_id=(ta, ba_peer(k)), device_id_type=MESH,
-        )
-        for k in range(1, NBA)
-    ]
-    for copy in basis_sends:
-        copy.start()
-
-    local_part(0)
+    core = lax.rem(ta, 2)
+    z_place, x_place = ba // 2, lax.rem(ba, 2)
+    piece_rows = GROUP * COMPS // PIECES
+    queue = [(step, piece) for step in range(NBA - 1) for piece in range(PIECES)]
+
+    def send_basis(count):
+        for step, piece in queue[:count]:
+            (z_even, x_even_core), (z_odd, x_odd_core) = ORDER[0][step], ORDER[1][step]
+            dz = jnp.where(core == 0, z_even, z_odd)
+            dx = jnp.where(core == 0, x_even_core, x_odd_core)
+            to = lax.rem(z_place + dz, NBA // 2) * 2 + lax.rem(x_place + dx, 2)
+            start = pl.multiple_of(ba * (GROUP * COMPS) + piece * piece_rows, 8)
+            pltpu.make_async_remote_copy(
+                src_ref=basis.at[pl.ds(piece * piece_rows, piece_rows), to],
+                dst_ref=basis_all.at[pl.ds(start, piece_rows)],
+                send_sem=bs, recv_sem=br.at[ba],
+                device_id=(ta, to), device_id_type=MESH,
+            ).start()
+        del queue[:count]
+
+    send_basis(PACE[0])
     for copy in first_halo:
         copy.wait_recv()
+    send_basis(PACE[1])
     time_finish(0)
     time_prepare(1)
     second_halo = halo_copies(1)
     for copy in second_halo:
         copy.start()
+    send_basis(PACE[2])
     local_part(1)
+    send_basis(PACE[3])
     for copy in second_halo:
         copy.wait_recv()
     time_finish(1)
@@ -316,6 +336,7 @@
     ]
     for copy in applied_sends:
         copy.start()
+    send_basis(PACE[4])
     pltpu.make_async_copy(psi.at[2, :, ba], block_of(a_all, ba, MINE * COMPS), ar.at[ba]).start()
     cm[...] = jnp.zeros_like(cm)
     for k in range(NBA):
@@ -362,35 +383,28 @@
 
     lax.fori_loop(0, NBA, basis_chunk, 0)
 
+    def all_of(ref, sem):
+        pltpu.make_async_copy(ref, ref, sem).wait()
+
     c_part[...] = cm[...].T[0 : 2 * BLOCK]
-    corr_sends = [
+    for k in range(1, NBA):
         pltpu.make_async_remote_copy(
-            src_ref=c_part, dst_ref=c_ba.at[ba], send_sem=cs1.at[k], recv_sem=cr1.at[ba],
+            src_ref=c_part, dst_ref=c_ba.at[ba], send_sem=cs.at[0], recv_sem=cr.at[0],
             device_id=(ta, ba_peer(k)), device_id_type=MESH,
-        )
-        for k in range(1, NBA)
-    ]
-    for copy in corr_sends:
-        copy.start()
+        ).start()
     c_ba[ba] = c_part[...]
-    for k in range(1, NBA):
-        pltpu.make_async_copy(c_ba.at[ba_peer(k)], c_ba.at[ba_peer(k)], cr1.at[ba_peer(k)]).wait()
+    all_of(c_ba.at[pl.ds(0, NBA - 1)], cr.at[0])
     total = c_ba[0]
     for k in range(1, NBA):
         total = total + c_ba[k]
     c_sum[...] = total
-    more_sends = [
+    for k in range(1, NTA):
         pltpu.make_async_remote_copy(
-            src_ref=c_sum, dst_ref=c_ta.at[ta], send_sem=cs2.at[k], recv_sem=cr2.at[ta],
+            src_ref=c_sum, dst_ref=c_ta.at[ta], send_sem=cs.at[1], recv_sem=cr.at[1],
             device_id=(ta_peer(k), ba), device_id_type=MESH,
-        )
-        for k in range(1, NTA)
-    ]
-    for copy in more_sends:
-        copy.start()
+        ).start()
     c_ta[ta] = c_sum[...]
-    for k in range(1, NTA):
-        pltpu.make_async_copy(c_ta.at[ta_peer(k)], c_ta.at[ta_peer(k)], cr2.at[ta_peer(k)]).wait()
+    all_of(c_ta.at[pl.ds(0, NTA - 1)], cr.at[1])
     total = c_ta[0]
     for k in range(1, NTA):
         total = total + c_ta[k]
@@ -427,39 +441,29 @@
     both = upper + turned
     g_part[...] = jnp.where(lane < 32, both[0:8], lroll(both[8:16], 32))
 
-    gram_sends = [
+    for k in range(1, NTA):
         pltpu.make_async_remote_copy(
-            src_ref=g_part, dst_ref=g_ta.at[ta], send_sem=gs1.at[k], recv_sem=gr1.at[ta],
+            src_ref=g_part, dst_ref=g_ta.at[ta], send_sem=gs1, recv_sem=gr1,
             device_id=(ta_peer(k), ba), device_id_type=MESH,
-        )
-        for k in range(1, NTA)
-    ]
-    for copy in gram_sends:
-        copy.start()
+        ).start()
     g_ta[ta] = g_part[...]
+    mine = pl.ds(pl.multiple_of(ba * GROUP, GROUP), GROUP)
     c_full[2 * BLOCK : LANES] = jnp.zeros((LANES - 2 * BLOCK, KEPT), F32)
     cm[...] = c_full[...].T
-    mine = pl.ds(pl.multiple_of(ba * GROUP, GROUP), GROUP)
     corr[0] = cm[mine, 0:BLOCK]
     corr[1] = cm[mine, BLOCK : 2 * BLOCK]
-    for k in range(1, NTA):
-        pltpu.make_async_copy(g_ta.at[ta_peer(k)], g_ta.at[ta_peer(k)], gr1.at[ta_peer(k)]).wait()
+    all_of(g_ta.at[pl.ds(0, NTA - 1)], gr1)
     total = g_ta[0]
     for k in range(1, NTA):
         total = total + g_ta[k]
     g_sum[...] = total
-    gram_more = [
+    for k in range(1, NBA):
         pltpu.make_async_remote_copy(
-            src_ref=g_sum, dst_ref=g_ba.at[ba], send_sem=gs2.at[k], recv_sem=gr2.at[ba],
+            src_ref=g_sum, dst_ref=g_ba.at[ba], send_sem=gs2, recv_sem=gr2,
             device_id=(ta, ba_peer(k)), device_id_type=MESH,
-        )
-        for k in range(1, NBA)
-    ]
-    for copy in gram_more:
-        copy.start()
+        ).start()
     g_ba[ba] = g_sum[...]
-    for k in range(1, NBA):
-        pltpu.make_async_copy(g_ba.at[ba_peer(k)], g_ba.at[ba_peer(k)], gr2.at[ba_peer(k)]).wait()
+    all_of(g_ba.at[pl.ds(0, NBA - 1)], gr2)
     total = g_ba[0]
     for k in range(1, NBA):
         total = total + g_ba[k]
@@ -496,21 +500,21 @@
                 part = ortho[ri * BLOCK : (ri + 1) * BLOCK, offset : offset + LANES]
                 osend[pl.ds(ri * PLANES + plane, BLOCK, stride=COMPS), :] = part
 
-    out_sends = [
+    for k in range(1, NBA):
         pltpu.make_async_remote_copy(
             src_ref=block_of(osend, ba_peer(k), MINE * COMPS), dst_ref=out.at[:, ba],
-            send_sem=os_.at[k], recv_sem=or_.at[ba],
+            send_sem=os_, recv_sem=or_.at[ba],
             device_id=(ta, ba_peer(k)), device_id_type=MESH,
-        )
-        for k in range(1, NBA)
-    ]
-    for copy in out_sends:
-        copy.start()
+        ).start()
     pltpu.make_async_copy(block_of(osend, ba, MINE * COMPS), out.at[:, ba], or_.at[ba]).start()
-    for copy in (*first_halo, *second_halo, *basis_sends, *applied_sends, *corr_sends, *more_sends):
+    for copy in (*first_halo, *second_halo, *applied_sends):
         copy.wait_send()
-    for copy in (*gram_sends, *gram_more, *out_sends):
-        copy.wait_send()
+    all_of(basis_all.at[pl.ds(0, (NBA - 1) * GROUP * COMPS)], bs)
+    all_of(c_ba.at[pl.ds(0, NBA - 1)], cs.at[0])
+    all_of(c_ta.at[pl.ds(0, NTA - 1)], cs.at[1])
+    all_of(g_ta.at[pl.ds(0, NTA - 1)], gs1)
+    all_of(g_ba.at[pl.ds(0, NBA - 1)], gs2)
+    all_of(osend.at[pl.ds(0, (NBA - 1) * MINE * COMPS)], os_)
     for k in range(NBA):
         place = block_of(osend, ba_peer(k), MINE * COMPS)
         pltpu.make_async_copy(place, out.at[:, ba_peer(k)], or_.at[ba_peer(k)]).wait()
@@ -554,8 +558,8 @@
         vmem((two, 2 * WIDE), BF16),
         vmem((KEPT, LANES), F32),
         vmem((two, KEPT), F32),
+        vmem((two, KEPT), F32),
         vmem((NBA, two, KEPT), F32),
-        vmem((two, KEPT), F32),
         vmem((NTA, two, KEPT), F32),
         vmem((LANES, KEPT), F32),
         vmem((2 * two, 2 * KEPT), BF16),
@@ -568,9 +572,8 @@
         vmem((two, LANES), F32),
         vmem((BLOCK * COMPS, LANES), F32),
         dma((3,)), dma((2, 2)), dma((2, 2)),
-        dma((NBA,)), dma((NBA,)), dma((NBA,)), dma((NBA,)), dma((NBA,)), dma((NBA,)),
-        dma((NTA,)), dma((NTA,)), dma((NTA,)), dma((NTA,)),
-        dma((NBA,)), dma((NBA,)), dma((NBA,)), dma((NBA,)),
+        dma, dma((NBA,)), dma((NBA,)), dma((NBA,)), dma((2,)), dma((2,)),
+        dma, dma, dma, dma, dma, dma((NBA,)),
     ]
     ortho, correlations = pl.pallas_call(
         kernel,

time: 67.9 us -> 64.8 us (0.954)
  Pallas kernels: 64.2 us -> 61 us
    pallas_call x1, Pallas kernels: 64.2 us -> 61 us  [per_device(): pl.pallas_call(kernel, out_shape=(jax.ShapeDtypeStruct((MINE * COMPS, 8,...]
where the time goes in v2:
time: 64.8 us; the launch traced here: 64.6 us
  Pallas kernels  61 us (94%)
  local copies, waits for them, and re-layouts  2.94 us (5%)
    pallas_call x1, Pallas kernels, per_device(): pl.pallas_call(kernel, out_shape=(jax.ShapeDtypeStruct((MINE * COMPS, 8,...  61 us
    unnamed x2, local copies, waits for them, and re-layouts  2.94 us

profile of v2, /device:TPU:0, one launch (start us, length us, event | category | flops | bytes accessed | tf_op | source)
XLA Modules:
  0.0 64.6 jit_solution(17726639200150797834)
XLA Ops:
  0.6 61.0 %shard_map.59 = (f32[48,8,128]{2,1,0:T(8,128)}, f32[2,16,16]{2,1,0:T(8,128)}) custom-call(f32[384,8,128]{2,1,0:T(8,128)} %bitcast.25, f32[384,8,128]{2,1,0:T(8,128)} %bitcast.26, f32[72,8,128]{2,1,0:T(8,128)} %bitcast.28, f32[144,8,128]{2,1,0:T(8,128)} %bitcast.27), custom_call_target="tpu_custom_call" | custom-call | tf_op jit(solution)/shard_map/pallas_call | solution.py:578
  61.6 1.6 %copy.13 = f32[2,2,4,3,2,512]{5,4,3,2,1,0:T(2,128)} copy(f32[2,2,4,3,2,512]{5,4,3,2,1,0:T(2,128)} %bitcast.29) | data formatting | bytes 393216
  63.2 1.3 %copy.14 = f32[2,16,16]{2,1,0:T(8,128)} copy(f32[2,16,16]{2,1,0:T(8,128)} %get-tuple-element.9) | data formatting | bytes 4096

commit v3 on v2

--- a/solution.py
+++ b/solution.py
@@ -22,10 +22,11 @@
 
 PIECES = 2
 ORDER = (
-    ((1, 0), (0, 1), (3, 0), (1, 1), (2, 0), (3, 1), (2, 1)),
-    ((0, 1), (3, 0), (1, 1), (1, 0), (3, 1), (2, 1), (2, 0)),
+    ((2, 1), (2, 0), (1, 1), (3, 1), (1, 0), (3, 0), (0, 1)),
+    ((2, 0), (2, 1), (3, 1), (1, 1), (1, 0), (0, 1), (3, 0)),
 )
 PACE = (3, 0, 4, 0, 7)
+EARLY = 3
 
 ISIGMA = (
     ((1, True, 1), (0, True, 1)),
@@ -360,8 +361,23 @@
         x_lo[0:BLOCK, later] = im_lo
         x_lo[BLOCK : 2 * BLOCK, later] = -re_lo
 
+    def source_of(dz, dx):
+        return lax.rem(z_place + NBA // 2 - dz, NBA // 2) * 2 + lax.rem(x_place + dx, 2)
+
+    def packed(values, base):
+        codes = [sum(value * base**i for i, value in enumerate(row)) for row in values]
+        return jnp.where(core == 0, codes[0], codes[1])
+
+    steps = [((0, 0), *order) for order in ORDER]
+    z_codes = packed([[step[0] for step in order] for order in steps], 4)
+    x_codes = packed([[step[1] for step in order] for order in steps], 2)
+    places = packed([[steps[0].index(step) for step in order] for order in steps], 8)
+
     def basis_chunk(k, carry):
-        source = lax.rem(ba + k, NBA)
+        two_to = sum(jnp.where(k == i, 2**i, 0) for i in range(NBA))
+        dz = lax.rem(z_codes // (two_to * two_to), 4)
+        spot = lax.rem(places // (two_to * two_to * two_to), 8)
+        source = source_of(dz, lax.rem(x_codes // two_to, 2))
         place = block_of(basis_all, source, GROUP * COMPS)
         pltpu.make_async_copy(place, place, br.at[source]).wait()
         highs, lows = [], []
@@ -378,36 +394,52 @@
         low = jnp.concatenate(lows, axis=1)
         both = matmul(jnp.concatenate([high, low], axis=0), x_hi[...], NT_DIMS)
         total = both[0:GROUP] + both[GROUP : 2 * GROUP] + matmul(high, x_lo[...], NT_DIMS)
-        cm[pl.ds(pl.multiple_of(source * GROUP, GROUP), GROUP), 0 : 2 * BLOCK] = total
+        cm[0:GROUP, 0 : 2 * BLOCK] = total
+        shift = 64 * lax.rem(spot, 2)
+        upper, lower = cm[0:8], cm[8:16]
+        c_part[spot // 2] = c_part[spot // 2] + (pltpu.roll(upper, shift, 1) + pltpu.roll(lower, shift + 32, 1))
         return carry
-
-    lax.fori_loop(0, NBA, basis_chunk, 0)
 
     def all_of(ref, sem):
         pltpu.make_async_copy(ref, ref, sem).wait()
 
-    c_part[...] = cm[...].T[0 : 2 * BLOCK]
+    def send_tiles(first, count, sem):
+        tiles_of = pl.ds(first, count)
+        for k in range(1, NTA):
+            pltpu.make_async_remote_copy(
+                src_ref=c_part.at[tiles_of], dst_ref=c_ta.at[ta, tiles_of], send_sem=cs.at[sem], recv_sem=cr.at[sem],
+                device_id=(ta_peer(k), ba), device_id_type=MESH,
+            ).start()
+        c_ta[ta, tiles_of] = c_part[tiles_of]
+
+    c_part[...] = jnp.zeros_like(c_part)
+    lax.fori_loop(0, 2 * EARLY, basis_chunk, 0)
+    send_tiles(0, EARLY, 0)
+    lax.fori_loop(2 * EARLY, NBA, basis_chunk, 0)
+    send_tiles(EARLY, NBA // 2 - EARLY, 1)
+
+    for first, count, sem in ((0, EARLY, 0), (EARLY, NBA // 2 - EARLY, 1)):
+        all_of(c_ta.at[pl.ds(0, NTA - 1), pl.ds(first, count)], cr.at[sem])
+        for i in range(first, first + count):
+            total = c_ta[0, i]
+            for k in range(1, NTA):
+                total = total + c_ta[k, i]
+            for part in range(4):
+                source = source_of(*steps[0][2 * i + part // 2])
+                row = pl.multiple_of(source * GROUP + 8 * (part % 2), 8)
+                cm[pl.ds(row, 8)] = lroll(total, LANES - 32 * part) if part else total
+
+    c_sum[...] = cm[...].T[0 : 2 * BLOCK]
     for k in range(1, NBA):
         pltpu.make_async_remote_copy(
-            src_ref=c_part, dst_ref=c_ba.at[ba], send_sem=cs.at[0], recv_sem=cr.at[0],
+            src_ref=c_sum, dst_ref=c_ba.at[ba], send_sem=cs.at[2], recv_sem=cr.at[2],
             device_id=(ta, ba_peer(k)), device_id_type=MESH,
         ).start()
-    c_ba[ba] = c_part[...]
-    all_of(c_ba.at[pl.ds(0, NBA - 1)], cr.at[0])
+    c_ba[ba] = c_sum[...]
+    all_of(c_ba.at[pl.ds(0, NBA - 1)], cr.at[2])
     total = c_ba[0]
     for k in range(1, NBA):
         total = total + c_ba[k]
-    c_sum[...] = total
-    for k in range(1, NTA):
-        pltpu.make_async_remote_copy(
-            src_ref=c_sum, dst_ref=c_ta.at[ta], send_sem=cs.at[1], recv_sem=cr.at[1],
-            device_id=(ta_peer(k), ba), device_id_type=MESH,
-        ).start()
-    c_ta[ta] = c_sum[...]
-    all_of(c_ta.at[pl.ds(0, NTA - 1)], cr.at[1])
-    total = c_ta[0]
-    for k in range(1, NTA):
-        total = total + c_ta[k]
     norm = 1.0 / (24.0 * 512 * 2 * NTA)
     total = total * norm
     c_full[0 : 2 * BLOCK] = total
@@ -510,14 +542,20 @@
     for copy in (*first_halo, *second_halo, *applied_sends):
         copy.wait_send()
     all_of(basis_all.at[pl.ds(0, (NBA - 1) * GROUP * COMPS)], bs)
-    all_of(c_ba.at[pl.ds(0, NBA - 1)], cs.at[0])
-    all_of(c_ta.at[pl.ds(0, NTA - 1)], cs.at[1])
+    all_of(c_ta.at[pl.ds(0, NTA - 1), pl.ds(0, EARLY)], cs.at[0])
+    all_of(c_ta.at[pl.ds(0, NTA - 1), pl.ds(EARLY, NBA // 2 - EARLY)], cs.at[1])
+    all_of(c_ba.at[pl.ds(0, NBA - 1)], cs.at[2])
     all_of(g_ta.at[pl.ds(0, NTA - 1)], gs1)
     all_of(g_ba.at[pl.ds(0, NBA - 1)], gs2)
     all_of(osend.at[pl.ds(0, (NBA - 1) * MINE * COMPS)], os_)
     for k in range(NBA):
         place = block_of(osend, ba_peer(k), MINE * COMPS)
         pltpu.make_async_copy(place, out.at[:, ba_peer(k)], or_.at[ba_peer(k)]).wait()
+
+
+def hand_over(ortho_in, corr_in, ortho_out, corr_out):
+    ortho_out[...] = ortho_in[...]
+    corr_out[...] = corr_in[...]
 
 
 def tiles(array):
@@ -557,10 +595,10 @@
         vmem((two, 2 * WIDE), BF16),
         vmem((two, 2 * WIDE), BF16),
         vmem((KEPT, LANES), F32),
-        vmem((two, KEPT), F32),
+        vmem((NBA // 2, 8, LANES), F32),
         vmem((two, KEPT), F32),
         vmem((NBA, two, KEPT), F32),
-        vmem((NTA, two, KEPT), F32),
+        vmem((NTA, NBA // 2, 8, LANES), F32),
         vmem((LANES, KEPT), F32),
         vmem((2 * two, 2 * KEPT), BF16),
         vmem((two, WIDE), BF16),
@@ -572,7 +610,7 @@
         vmem((two, LANES), F32),
         vmem((BLOCK * COMPS, LANES), F32),
         dma((3,)), dma((2, 2)), dma((2, 2)),
-        dma, dma((NBA,)), dma((NBA,)), dma((NBA,)), dma((2,)), dma((2,)),
+        dma, dma((NBA,)), dma((NBA,)), dma((NBA,)), dma((3,)), dma((3,)),
         dma, dma, dma, dma, dma, dma((NBA,)),
     ]
     ortho, correlations = pl.pallas_call(
@@ -588,6 +626,15 @@
             collective_id=0, has_side_effects=True, vmem_limit_bytes=56 * 1024 * 1024
         ),
     )(tiles(search_block), tiles(kept_basis), tiles(gauge_links), tiles(clover_term))
+    ortho, correlations = pl.pallas_call(
+        hand_over,
+        out_shape=(
+            jax.ShapeDtypeStruct(ortho.shape, F32),
+            jax.ShapeDtypeStruct(correlations.shape, F32),
+        ),
+        in_specs=[in_vmem] * 2,
+        out_specs=(in_vmem, in_vmem),
+    )(ortho, correlations)
     slab = search_block.shape[-2:]
     return untiles(ortho, (MINE, 2, 4, 3, *slab)), correlations
 

time: 64.8 us -> 60.5 us (0.934)
  local copies, waits for them, and re-layouts: 2.94 us -> 0 us
  Pallas kernels: 61 us -> 59.7 us
    pallas_call x1, Pallas kernels: 61 us -> 58 us  [per_device(): pl.pallas_call(kernel, out_shape=(jax.ShapeDtypeStruct((MINE * COMPS, 8,...]
    unnamed x2 -> x0, local copies, waits for them, and re-layouts: 2.94 us -> none
    pallas_call x0 -> x1, Pallas kernels: none -> 1.62 us  [per_device(): pl.pallas_call(hand_over, out_shape=(jax.ShapeDtypeStruct(ortho.shape, F3...]
where the time goes in v3:
time: 60.5 us; the launch traced here: 60.3 us
  Pallas kernels  59.7 us (99%)
  between operations  0.64 us (1%)
    pallas_call x1, Pallas kernels, per_device(): pl.pallas_call(kernel, out_shape=(jax.ShapeDtypeStruct((MINE * COMPS, 8,...  58 us
    pallas_call x1, Pallas kernels, per_device(): pl.pallas_call(hand_over, out_shape=(jax.ShapeDtypeStruct(ortho.shape, F3...  1.62 us

profile of v3, /device:TPU:0, one launch (start us, length us, event | category | flops | bytes accessed | tf_op | source)
XLA Modules:
  0.0 60.3 jit_solution(16445828544999887253)
XLA Ops:
  0.6 58.0 %shard_map.59 = (f32[48,8,128]{2,1,0:T(8,128)}, f32[2,16,16]{2,1,0:T(8,128)}) custom-call(f32[384,8,128]{2,1,0:T(8,128)} %bitcast.25, f32[384,8,128]{2,1,0:T(8,128)} %bitcast.26, f32[72,8,128]{2,1,0:T(8,128)} %bitcast.28, f32[144,8,128]{2,1,0:T(8,128)} %bitcast.27), custom_call_target="tpu_custom_call" | custom-call | tf_op jit(solution)/shard_map/pallas_call | solution.py:616
  58.7 1.6 %shard_map.60 = (f32[48,8,128]{2,1,0:T(8,128)}, f32[2,16,16]{2,1,0:T(8,128)}) custom-call(f32[48,8,128]{2,1,0:T(8,128)} %get-tuple-element.6.ortho_in, f32[2,16,16]{2,1,0:T(8,128)} %get-tuple-element.7.corr_in), custom_call_target="tpu_custom_call" | custom-call | tf_op jit(solution)/shard_map/pallas_call | solution.py:629
